TPU v7x, 32 devices: a whole 2x2x4 slice. The times are simulated.
32 devices in a mesh: dp: 8 (over z, y), tensor: 4 (over x, core).
Axes of the slice: x: 2, y: 2, z: 4, core: 2. Of those that a mesh axis runs over, the one named last changes fastest.
Arguments:
- tokens: bfloat16 [12288, 768], P('dp'), may hold values from -6 to 6
- segment_ids: int32 [24, 512], P('dp'), may hold values from 0 to 16, as said below
- prev_scores: bfloat16 [24, 12, 512, 512], P('dp', 'tensor'), may hold values from -6 to 6
- out_grad: bfloat16 [12288, 768], P('dp'), may hold values from -6 to 6
- attn_in_master: float32 [3, 768, 768], P(None, 'dp', 'tensor'), may hold values from -0.21875 to 0.21875
- attn_out_master: float32 [768, 768], P('tensor', 'dp'), may hold values from -0.875 to 0.875
- ffn_in_master: float32 [768, 3072], P('dp', 'tensor'), may hold values from -0.21875 to 0.21875
- ffn_out_master: float32 [3072, 768], P('tensor', 'dp'), may hold values from -0.109375 to 0.109375
- attn_in_first: float32 [3, 768, 768], P(None, 'dp', 'tensor'), may hold values from -0.0024414062 to 0.0024414062
- attn_out_first: float32 [768, 768], P('tensor', 'dp'), may hold values from -0.0024414062 to 0.0024414062
- ffn_in_first: float32 [768, 3072], P('dp', 'tensor'), may hold values from -0.0024414062 to 0.0024414062
- ffn_out_first: float32 [3072, 768], P('tensor', 'dp'), may hold values from -0.0024414062 to 0.0024414062
- attn_in_second: float32 [3, 768, 768], P(None, 'dp', 'tensor'), may hold values from 1.4110135e-07 to 5.644054e-07
- attn_out_second: float32 [768, 768], P('tensor', 'dp'), may hold values from 1.4110135e-07 to 5.644054e-07
- ffn_in_second: float32 [768, 3072], P('dp', 'tensor'), may hold values from 1.4110135e-07 to 5.644054e-07
- ffn_out_second: float32 [3072, 768], P('tensor', 'dp'), may hold values from 1.4110135e-07 to 5.644054e-07
- qv_bias: float32 [2, 768], P(None, 'tensor'), may hold values from -1.75 to 1.75
- ffn_bias: float32 [3072], P('tensor'), may hold values from -1.75 to 1.75
- row_params: float32 [6, 768], replicated, may hold values from -0.75 to 1.65, as said below
- qv_bias_first: float32 [2, 768], P(None, 'tensor'), may hold values from -0.009765625 to 0.009765625
- ffn_bias_first: float32 [3072], P('tensor'), may hold values from -0.0024414062 to 0.0024414062
- row_params_first: float32 [6, 768], replicated, may hold values from -0.009765625 to 0.009765625
- qv_bias_second: float32 [2, 768], P(None, 'tensor'), may hold values from 2.2576216e-06 to 9.030487e-06
- ffn_bias_second: float32 [3072], P('tensor'), may hold values from 7.0550676e-08 to 2.822027e-07
- row_params_second: float32 [6, 768], replicated, may hold values from 2.2576216e-06 to 9.030487e-06
Outputs:
- out_tokens: bfloat16 [12288, 768], P('dp')
- tokens_grad: float32 [12288, 768], P('dp')
- scores_grad: float32 [24, 12, 512, 512], P('dp', 'tensor')
- grad_norm: float32 [], replicated
- attn_in_new: float32 [3, 768, 768], P(None, 'dp', 'tensor')
- attn_out_new: float32 [768, 768], P('tensor', 'dp')
- ffn_in_new: float32 [768, 3072], P('dp', 'tensor')
- ffn_out_new: float32 [3072, 768], P('tensor', 'dp')
- attn_in_first_new: float32 [3, 768, 768], P(None, 'dp', 'tensor')
- attn_out_first_new: float32 [768, 768], P('tensor', 'dp')
- ffn_in_first_new: float32 [768, 3072], P('dp', 'tensor')
- ffn_out_first_new: float32 [3072, 768], P('tensor', 'dp')
- attn_in_second_new: float32 [3, 768, 768], P(None, 'dp', 'tensor')
- attn_out_second_new: float32 [768, 768], P('tensor', 'dp')
- ffn_in_second_new: float32 [768, 3072], P('dp', 'tensor')
- ffn_out_second_new: float32 [3072, 768], P('tensor', 'dp')
- attn_in_copy: bfloat16 [3, 768, 768], P(None, 'dp', 'tensor')
- attn_out_copy: bfloat16 [768, 768], P('tensor', 'dp')
- ffn_in_copy: bfloat16 [768, 3072], P('dp', 'tensor')
- ffn_out_copy: bfloat16 [3072, 768], P('tensor', 'dp')
- qv_bias_new: float32 [2, 768], P(None, 'tensor')
- ffn_bias_new: float32 [3072], P('tensor')
- row_params_new: float32 [6, 768], replicated
- qv_bias_first_new: float32 [2, 768], P(None, 'tensor')
- ffn_bias_first_new: float32 [3072], P('tensor')
- row_params_first_new: float32 [6, 768], replicated
- qv_bias_second_new: float32 [2, 768], P(None, 'tensor')
- ffn_bias_second_new: float32 [3072], P('tensor')
- row_params_second_new: float32 [6, 768], replicated
Inputs may be any that keep to these rules, and one draw needn't show every extreme that they name: `segment_ids`: in each pack, live slots come first and empty slots (0) last; live ids start at 1 and rise by one from one sequence to the next; sequences start at multiples of 32 slots; a pack holds 128, 256, 384 or 512 live slots; the first pack holds one sequence of 512 slots, the second pack 3 * 128 live slots, the last pack 16 sequences of 32 slots. `row_params`: rows 0 and 1 lie between 0.35 and 1.65.
All inputs are finite; a program needn't handle non-finite values.
Results may differ from a plain program's by a relative error of at most 0.012.
The roundings to bfloat16 on the way count: a program that leaves them out, or rounds other values in their place, can miss the bound.
Values may be sent and summed in bfloat16 or wider, within the bound.
A program may use at most 128 MiB of HBM per device.

v0:
```python
from functools import partial
import jax
import jax.numpy as jnp
from jax import lax
from jax.sharding import PartitionSpec as P

D = 768
STEP = 5
beta_one = 0.5
beta_two = 0.5
weight_decay = 0.01
adam_eps = 1e-08
norm_eps = 1e-06
small_rate = 0.5


def layer_norm(rows_in, gain_row, shift_row):
    row_mean = jnp.mean(rows_in, axis=-1, keepdims=True)
    centred = rows_in - row_mean
    spread = jnp.mean(centred * centred, axis=-1, keepdims=True)
    return centred * lax.rsqrt(spread + norm_eps) * gain_row + shift_row


def masked_scores(scale, query_heads, key_heads, prev_block, seg_ids):
    same_seq = seg_ids[:, None] == seg_ids[None, :]
    scores = jnp.einsum(
        "qhe,khe->hqk", query_heads, key_heads, preferred_element_type=jnp.float32
    ) * scale + prev_block.astype(jnp.float32)
    return jnp.where(same_seq[None], scores, -1000000000.0)


def attend(scale, pieces):
    query_heads, key_heads, value_heads, prev_block, seg_ids = pieces
    scores = masked_scores(scale, query_heads, key_heads, prev_block, seg_ids)
    row_top = jnp.max(scores, axis=-1, keepdims=True)
    expo = jnp.exp(scores - row_top)
    row_total = jnp.sum(expo, axis=-1, keepdims=True)
    weights_low = (expo / row_total).astype(jnp.bfloat16)
    context_heads = jnp.einsum(
        "hqk,khe->qhe", weights_low, value_heads, preferred_element_type=jnp.float32
    )
    return (context_heads.astype(jnp.bfloat16), row_top + jnp.log(row_total))


def attend_back(scale, pieces):
    query_heads, key_heads, value_heads, prev_block, seg_ids, row_lse, grad_heads = pieces
    scores = masked_scores(scale, query_heads, key_heads, prev_block, seg_ids)
    soft = jnp.exp(scores - row_lse)
    soft_low = soft.astype(jnp.bfloat16)
    grad_soft = jnp.einsum(
        "qhe,khe->hqk", grad_heads, value_heads, preferred_element_type=jnp.float32
    )
    row_dot = jnp.sum(soft * grad_soft, axis=-1, keepdims=True)
    score_grad = (soft * (grad_soft - row_dot)).astype(jnp.bfloat16)
    grad_query = (
        jnp.einsum("hqk,khe->qhe", score_grad, key_heads, preferred_element_type=jnp.float32)
        * scale
    ).astype(jnp.bfloat16)
    grad_key = (
        jnp.einsum("hqk,qhe->khe", score_grad, query_heads, preferred_element_type=jnp.float32)
        * scale
    ).astype(jnp.bfloat16)
    grad_value = jnp.einsum(
        "hqk,qhe->khe", soft_low, grad_heads, preferred_element_type=jnp.float32
    ).astype(jnp.bfloat16)
    return (grad_query, grad_key, grad_value, score_grad.astype(jnp.float32))


def adam_update(weight, gradient, first_moment, second_moment, decay_rate, learn_rate):
    first_new = beta_one * first_moment + (1.0 - beta_one) * gradient
    second_new = beta_two * second_moment + (1.0 - beta_two) * gradient * gradient
    corrected = (
        first_new
        / (1.0 - beta_one**STEP)
        / (jnp.sqrt(second_new / (1.0 - beta_two**STEP)) + adam_eps)
    )
    return (weight - learn_rate * (corrected + decay_rate * weight), first_new, second_new)


def on_device(
    tokens,
    segment_ids,
    prev_scores,
    out_grad,
    attn_in_master,
    attn_out_master,
    ffn_in_master,
    ffn_out_master,
    attn_in_first,
    attn_out_first,
    ffn_in_first,
    ffn_out_first,
    attn_in_second,
    attn_out_second,
    ffn_in_second,
    ffn_out_second,
    qv_bias,
    ffn_bias,
    row_params,
    qv_bias_first,
    ffn_bias_first,
    row_params_first,
    qv_bias_second,
    ffn_bias_second,
    row_params_second,
):
    attn_in, attn_out, ffn_in, ffn_out = (
        lax.all_gather(attn_in_master.astype(jnp.bfloat16), "dp", axis=1, tiled=True),
        lax.all_gather(attn_out_master.astype(jnp.bfloat16), "dp", axis=1, tiled=True),
        lax.all_gather(ffn_in_master.astype(jnp.bfloat16), "dp", axis=0, tiled=True),
        lax.all_gather(ffn_out_master.astype(jnp.bfloat16), "dp", axis=1, tiled=True),
    )
    pack_count, pack_len = segment_ids.shape
    head_count = prev_scores.shape[1]
    head_width = attn_in.shape[2] // head_count
    scale = head_width ** (-0.5)
    token_count = tokens.shape[0]
    dp_count = lax.axis_size("dp")
    tensor_count = lax.axis_size("tensor")

    def split_heads(matrix):
        return matrix.reshape(pack_count, pack_len, head_count, head_width)

    projected = jnp.einsum("td,cde->cte", tokens, attn_in, preferred_element_type=jnp.float32)
    query_rows = (projected[0] + qv_bias[0]).astype(jnp.bfloat16)
    key_rows = projected[1].astype(jnp.bfloat16)
    value_rows = (projected[2] + qv_bias[1]).astype(jnp.bfloat16)
    query_heads = split_heads(query_rows)
    key_heads = split_heads(key_rows)
    value_heads = split_heads(value_rows)
    context_heads, row_lse = lax.map(
        partial(attend, scale), (query_heads, key_heads, value_heads, prev_scores, segment_ids)
    )
    context = context_heads.reshape(token_count, -1)
    attn_partial = jnp.dot(context, attn_out, preferred_element_type=jnp.float32)
    live_whole = (segment_ids > 0).astype(jnp.float32).reshape(token_count, 1)
    rows_start = tokens.astype(jnp.float32)
    attended = lax.psum(attn_partial, "tensor") + row_params[2]
    cotangent = out_grad.astype(jnp.float32)
    residual_one = rows_start + attended
    normed, first_pull = jax.vjp(layer_norm, residual_one, row_params[0], row_params[3])
    normed_low = normed.astype(jnp.bfloat16)
    pre_act = jnp.dot(normed_low, ffn_in, preferred_element_type=jnp.float32) + ffn_bias
    activation, gelu_pull = jax.vjp(partial(jax.nn.gelu, approximate=False), pre_act)
    act_low = activation.astype(jnp.bfloat16)
    ffn_partial = jnp.dot(act_low, ffn_out, preferred_element_type=jnp.float32)
    ffn_output = lax.psum(ffn_partial, "tensor") + row_params[4]

    def final_norm(rows_in, gain_row, shift_row):
        return layer_norm(rows_in, gain_row, shift_row) * live_whole

    final_rows, second_pull = jax.vjp(final_norm, normed + ffn_output, row_params[1], row_params[5])
    final_low = final_rows.astype(jnp.bfloat16)
    grad_res_two, grad_gain_two, grad_shift_two = second_pull(cotangent)
    grad_ffn_low = grad_res_two.astype(jnp.bfloat16)
    grad_ffn_out_bias = jnp.sum(grad_ffn_low.astype(jnp.float32), axis=0)
    grad_ffn_out = jnp.einsum(
        "tf,td->fd", act_low, grad_ffn_low, preferred_element_type=jnp.float32
    )
    grad_act = jnp.einsum("td,fd->tf", grad_ffn_low, ffn_out, preferred_element_type=jnp.float32)
    (grad_pre,) = gelu_pull(grad_act)
    grad_pre_low = grad_pre.astype(jnp.bfloat16)
    grad_ffn_bias = jnp.sum(grad_pre_low.astype(jnp.float32), axis=0)
    grad_ffn_in = jnp.einsum(
        "td,tf->df", normed_low, grad_pre_low, preferred_element_type=jnp.float32
    )
    hidden_part = jnp.einsum("tf,df->td", grad_pre_low, ffn_in, preferred_element_type=jnp.float32)
    grad_normed = grad_res_two + lax.psum(hidden_part, "tensor")
    grad_res_one, grad_gain_one, grad_shift_one = first_pull(grad_normed)
    att_low = grad_res_one.astype(jnp.bfloat16)
    grad_att_bias = jnp.sum(att_low.astype(jnp.float32), axis=0)
    grad_attn_out = jnp.einsum("te,td->ed", context, att_low, preferred_element_type=jnp.float32)
    grad_context = jnp.einsum(
        "td,ed->te", att_low, attn_out, preferred_element_type=jnp.float32
    ).astype(jnp.bfloat16)
    grad_query, grad_key, grad_value, scores_grad = lax.map(
        partial(attend_back, scale),
        (
            query_heads,
            key_heads,
            value_heads,
            prev_scores,
            segment_ids,
            row_lse,
            split_heads(grad_context),
        ),
    )
    grad_proj = jnp.stack(
        [
            grad_query.reshape(token_count, -1),
            grad_key.reshape(token_count, -1),
            grad_value.reshape(token_count, -1),
        ]
    )
    grad_attn_in = jnp.einsum("td,cte->cde", tokens, grad_proj, preferred_element_type=jnp.float32)
    grad_qv_bias = jnp.stack(
        [
            jnp.sum(grad_proj[0].astype(jnp.float32), axis=0),
            jnp.sum(grad_proj[2].astype(jnp.float32), axis=0),
        ]
    )
    input_part = jnp.einsum("cte,cde->td", grad_proj, attn_in, preferred_element_type=jnp.float32)
    norm_stack = jnp.stack([grad_gain_one, grad_gain_two, grad_shift_one, grad_shift_two])
    tokens_grad = grad_res_one + lax.psum(input_part, "tensor")
    grad_rows = jnp.stack(
        [
            norm_stack[0],
            norm_stack[1],
            grad_att_bias,
            norm_stack[2],
            grad_ffn_out_bias,
            norm_stack[3],
        ]
    )
    summed = lax.psum(
        (
            grad_attn_in,
            grad_attn_out,
            grad_ffn_in,
            grad_ffn_out,
            grad_qv_bias,
            grad_ffn_bias,
            grad_rows,
        ),
        "dp",
    )
    dp_index = lax.axis_index("dp")

    def own_part(whole_grad, shard, along):
        extent = shard.shape[along]
        return lax.dynamic_slice_in_dim(whole_grad, dp_index * extent, extent, along)

    shares = (
        own_part(summed[0], attn_in_master, 1),
        own_part(summed[1], attn_out_master, 1),
        own_part(summed[2], ffn_in_master, 0),
        own_part(summed[3], ffn_out_master, 1),
    )
    small_sums = (summed[4], summed[5], summed[6])
    local_squares = jnp.float32(0.0)
    for share in shares:
        local_squares = local_squares + jnp.sum(share * share)
    local_squares = (
        local_squares
        + (jnp.sum(small_sums[0] * small_sums[0]) + jnp.sum(small_sums[1] * small_sums[1]))
        / dp_count
    )
    local_squares = local_squares + jnp.sum(small_sums[2] * small_sums[2]) / (
        dp_count * tensor_count
    )
    total_squares = lax.psum(local_squares, ("dp", "tensor"))
    grad_norm = jnp.sqrt(total_squares)
    factor = 1.0 / jnp.maximum(grad_norm, 1.0)
    olds = (
        attn_in_master,
        attn_out_master,
        ffn_in_master,
        ffn_out_master,
        qv_bias,
        ffn_bias,
        row_params,
    )
    firsts = (
        attn_in_first,
        attn_out_first,
        ffn_in_first,
        ffn_out_first,
        qv_bias_first,
        ffn_bias_first,
        row_params_first,
    )
    seconds = (
        attn_in_second,
        attn_out_second,
        ffn_in_second,
        ffn_out_second,
        qv_bias_second,
        ffn_bias_second,
        row_params_second,
    )
    gradients = (
        shares[0],
        shares[1],
        shares[2],
        shares[3],
        small_sums[0],
        small_sums[1],
        small_sums[2],
    )
    decays = (weight_decay, weight_decay, weight_decay, weight_decay, 0.0, 0.0, 0.0)
    big_rate = D ** (-0.5)
    rates = (big_rate, big_rate, big_rate, big_rate, small_rate, small_rate, small_rate)
    updated = [
        adam_update(
            olds[place],
            gradients[place] * factor,
            firsts[place],
            seconds[place],
            decays[place],
            rates[place],
        )
        for place in range(7)
    ]
    return (
        final_low,
        tokens_grad,
        scores_grad,
        grad_norm,
        updated[0][0],
        updated[1][0],
        updated[2][0],
        updated[3][0],
        updated[0][1],
        updated[1][1],
        updated[2][1],
        updated[3][1],
        updated[0][2],
        updated[1][2],
        updated[2][2],
        updated[3][2],
        updated[0][0].astype(jnp.bfloat16),
        updated[1][0].astype(jnp.bfloat16),
        updated[2][0].astype(jnp.bfloat16),
        updated[3][0].astype(jnp.bfloat16),
        updated[4][0],
        updated[5][0],
        updated[6][0],
        updated[4][1],
        updated[5][1],
        updated[6][1],
        updated[4][2],
        updated[5][2],
        updated[6][2],
    )


def solution(mesh):
    in_specs = (
        P("dp", None),
        P("dp", None),
        P("dp", "tensor", None, None),
        P("dp", None),
        P(None, "dp", "tensor"),
        P("tensor", "dp"),
        P("dp", "tensor"),
        P("tensor", "dp"),
        P(None, "dp", "tensor"),
        P("tensor", "dp"),
        P("dp", "tensor"),
        P("tensor", "dp"),
        P(None, "dp", "tensor"),
        P("tensor", "dp"),
        P("dp", "tensor"),
        P("tensor", "dp"),
        P(None, "tensor"),
        P("tensor"),
        P(),
        P(None, "tensor"),
        P("tensor"),
        P(),
        P(None, "tensor"),
        P("tensor"),
        P(),
    )
    out_specs = (
        P("dp", None),
        P("dp", None),
        P("dp", "tensor", None, None),
        P(),
        P(None, "dp", "tensor"),
        P("tensor", "dp"),
        P("dp", "tensor"),
        P("tensor", "dp"),
        P(None, "dp", "tensor"),
        P("tensor", "dp"),
        P("dp", "tensor"),
        P("tensor", "dp"),
        P(None, "dp", "tensor"),
        P("tensor", "dp"),
        P("dp", "tensor"),
        P("tensor", "dp"),
        P(None, "dp", "tensor"),
        P("tensor", "dp"),
        P("dp", "tensor"),
        P("tensor", "dp"),
        P(None, "tensor"),
        P("tensor"),
        P(),
        P(None, "tensor"),
        P("tensor"),
        P(),
        P(None, "tensor"),
        P("tensor"),
        P(),
    )
    return jax.shard_map(
        on_device, mesh=mesh, in_specs=in_specs, out_specs=out_specs, check_vma=False
    )
```

profile of v0, /device:TPU:0, one launch (start us, length us, event | category | flops | bytes accessed | tf_op | source)
XLA Modules:
  0.0 938.5 jit_solution(11996233657050409264)
XLA Ops:
  9.2 38.6 %all_gather.12 = bf16[3,768,192]{2,0,1:T(4,128)(2,1)S(1)} all-gather(bf16[3,96,192]{2,0,1:T(4,128)(2,1)S(1)} %copy.141), channel_id=1, replica_groups=mesh['dp'=8,'tensor'=4] {'dp'}, dimensions={1}, use_global_device_ids=true | all-gather | bytes 995328 | tf_op jit(solution)/shard_map/all_gather | solution.py:108
  47.8 4.4 convolution_bitcast_fusion.1
  53.4 1.9 squeeze.37
  60.5 6.6 copy.146
  67.2 14.8 %while.28 = (s32[]{:T(128)}, bf16[3,512,3,64]{1,3,2,0:T(8,128)(2,1)S(1)}, f32[3,3,512,1]{2,1,3,0:T(4,128)S(1)}, bf16[3,512,3,64]{1,3,2,0:T(8,128)(2,1)}, s32[3,5...) while((s32[]{:T(128)}, ...), condition=%wide.region_3.4_spmd, body=%wide.region_0.3_spmd.sunk | while | flops 209549824 | bytes 12388973 | solution.py:131
  67.4 2.6 fusion.143
  72.4 2.6 fusion.143
  77.3 2.6 fusion.143
  82.7 31.0 %all_gather.13 = bf16[192,768]{0,1:T(8,128)(2,1)S(1)} all-gather(bf16[192,96]{0,1:T(8,128)(2,1)S(1)} %copy.148), channel_id=1, replica_groups=mesh['dp'=8,'tensor'=4] {'dp'}, dimensions={1}, use_global_device_ids=true | all-gather | bytes 331776 | tf_op jit(solution)/shard_map/all_gather | solution.py:109
  113.7 3.0 fusion.98
  116.8 1.6 convert_element_type.135
  118.5 1.6 convert_element_type.137
  120.5 89.9 %all-reduce.8.cloned.1.call-done = f32[1536,768]{1,0:T(8,128)} async-done(((f32[1536,768]{1,0:T(8,128)}), f32[1536,768]{1,0:T(8,128)}) %all-reduce.8.cloned.1.call-update) | async-done | bytes 4718608 | tf_op jit(solution)/shard_map/psum | solution.py:138
  210.4 3.0 fusion.95
  216.7 14.5 %multiply_convert_fusion.2 = (bf16[1536,768]{1,0:T(8,128)(2,1)}, f32[1536,768]{1,0:T(8,128)}, f32[1536,768]{1,0:T(8,128)}) fusion(f32[768]{0:T(1024)S(1)} %copy-done.28, bf16[1536,768]{1,0:T(8,128)(2,1)S(1)} %fusion.62, bf16[768,768]{1,0:T(8,128)(2,1)} %all-gather.3.cloned.1.call-done), kind=kOutput, calls=%fused_computation.82 | convolution fusion | flops 1889796096 | bytes 15338496 | tf_op jit(solution)/shard_map/dot_general | solution.py:143
  231.2 6.2 fusion.99
  237.7 94.0 %all-reduce.10.cloned.1.call-done = f32[1536,768]{1,0:T(8,128)} async-done(((f32[1536,768]{1,0:T(8,128)}), f32[1536,768]{1,0:T(8,128)}) %all-reduce.10.cloned.1.call-update) | async-done | bytes 4718608 | tf_op jit(solution)/shard_map/psum | solution.py:147
  331.7 4.7 fusion.93
  338.1 2.2 multiply_reduce_fusion.1
  340.4 3.8 fusion.92
  344.2 2.2 copy-done.2
  347.0 3.4 convert_reduce_fusion.2
  351.8 4.2 fusion.100
  356.1 5.3 fusion.102
  361.4 3.6 fusion.103
  365.0 85.4 %all-reduce.12.cloned.1.call-done = f32[1536,768]{1,0:T(8,128)} async-done(((f32[1536,768]{1,0:T(8,128)}), f32[1536,768]{1,0:T(8,128)}) %all-reduce.12.cloned.1.call-update) | async-done | bytes 4718608 | tf_op jit(solution)/shard_map/psum | solution.py:168
  450.3 6.7 multiply_reduce_fusion.2
  457.1 3.8 fusion.91
  468.6 55.0 %while.29 = (s32[]{:T(128)}, bf16[3,512,3,64]{1,3,2,0:T(8,128)(2,1)}, bf16[3,512,3,64]{1,3,2,0:T(8,128)(2,1)}, bf16[3,512,3,64]{1,3,2,0:T(8,128)(2,1)}, f32[3,3,...) while((s32[]{:T(128)}, ...), condition=%wide.region_17.18_spmd, body=%wide.region_15.17_spmd.sunk | while | flops 513505792 | bytes 43427472 | solution.py:176
  470.5 3.0 multiply_reduce_fusion.15
  473.5 2.6 bitcast_convert_fusion.2
  476.1 2.0 fusion.155
  478.1 2.2 fusion.156
  480.3 2.2 fusion.157
  482.5 2.4 copy.203
  484.9 2.0 constant_dynamic-update-slice_fusion.5
  486.9 1.6 fusion.154
  488.8 3.0 multiply_reduce_fusion.15
  491.8 2.6 bitcast_convert_fusion.2
  494.5 2.0 fusion.155
  496.5 2.2 fusion.156
  498.7 2.2 fusion.157
  500.9 2.4 copy.203
  503.3 2.0 constant_dynamic-update-slice_fusion.5
  507.1 3.0 multiply_reduce_fusion.15
  510.2 2.6 bitcast_convert_fusion.2
  512.8 2.0 fusion.155
  514.8 2.2 fusion.156
  517.0 2.2 fusion.157
  519.2 2.4 copy.203
  521.6 2.0 constant_dynamic-update-slice_fusion.5
  533.6 4.9 fusion.66
  540.5 4.5 convolution_bitcast_fusion
  548.2 39.3 %all-reduce = (f32[2,192]{1,0:T(2,128)S(1)}, f32[768]{0:T(1024)S(1)}, f32[6,768]{1,0:T(8,128)S(1)}) all-reduce(f32[2,192]{1,0:T(2,128)S(1)} %pad_maximum_fusion, f32[768]{0:T(1024)S(1)} %get-tuple-element.431, f32[6,768]{1,0:T(8,128)S(1)} %stack.31), channel_id=1, replica_groups=mesh['dp'=8,'tensor'=4] {'dp'}, use_global_device_ids=true, to_apply=%region_29.30 | all-reduce | flops 5760 | bytes 46080 | tf_op jit(solution)/shard_map/psum | solution.py:215
  591.2 183.0 %all-reduce.16.cloned.1.call-done = (f32[3,768,192]{1,2,0:T(8,128)}, f32[192,768]{1,0:T(8,128)}, f32[768,768]{1,0:T(8,128)}, f32[768,768]{0,1:T(8,128)}) async-done(((f32[3,768,192]{1,2,0:T(8,128)}, f32[192,768]{1,0:T(8,128)}, f32[768,768]{1,0:T(8,128)}, f32[768,768]{0,1:T(8,128)}), (f32[3,768,192]{1,2,0:T(8,128)}, f32[192,768]{1,0:T(8,128)}, f32[768,768]{1,0:T(8,128)}, ...) | async-done | bytes 7077904 | tf_op jit(solution)/shard_map/psum | solution.py:215
  775.8 1.8 multiply_reduce_fusion.9
  778.9 1.6 multiply_reduce_fusion.8
  781.2 1.7 multiply_reduce_fusion.7
  783.6 86.5 %all-reduce.14.cloned.1.call-done = f32[1536,768]{1,0:T(8,128)} async-done(((f32[1536,768]{1,0:T(8,128)}), f32[1536,768]{1,0:T(8,128)}) %all-reduce.14.cloned.1.call-update) | async-done | bytes 4718608 | tf_op jit(solution)/shard_map/psum | solution.py:204
  870.1 6.5 add_add_fusion.4
  876.6 39.5 %psum.95 = f32[]{:T(128)} all-reduce(f32[]{:T(128)S(6)} %add.314), channel_id=1, replica_groups=mesh['dp'=8,'tensor'=4] {'dp','tensor'}, use_global_device_ids=true, to_apply=%region_42.43 | all-reduce | flops 1 | bytes 8 | tf_op jit(solution)/shard_map/psum | solution.py:251
  921.8 1.9 fusion.87
  923.7 2.1 fusion.85
  925.8 2.2 fusion.83
  (201 shorter events, 59.4 us)
Async XLA Ops:
  8.0 202.4 %all-reduce.8.cloned.1.call-start = ((), (), s32[]{:S(2)}) async-start(), calls=%async_computation | async-start | bytes 9437184 | tf_op jit(solution)/shard_map/psum | solution.py:138
  47.8 4.4 copy-start.8
  52.2 3.2 copy-start.26
  60.5 6.7 copy-start.21
  67.2 15.5 %copy-start.13 = (f32[192,96]{1,0:T(8,128)S(1)}, f32[192,96]{1,0:T(8,128)}, u32[]{:S(2)}) copy-start(f32[192,96]{1,0:T(8,128)} %param.34) | copy-start | bytes 221188
  113.7 6.7 copy-start.22
  113.7 96.7 %copy-start.5 = (bf16[1536,768]{1,0:T(8,128)(2,1)S(1)}, bf16[1536,768]{1,0:T(8,128)(2,1)}, u32[]{:S(2)}) copy-start(bf16[1536,768]{1,0:T(8,128)(2,1)} %param.29) | copy-start | bytes 7077892
  116.8 99.9 %all-gather.3.cloned.1.call-start = ((), (), s32[]{:S(2)}) async-start(), calls=%async_computation.1 | async-start | bytes 1327104 | tf_op jit(solution)/shard_map/all_gather | solution.py:110
  118.5 112.7 %all-gather.5.cloned.1.call-start = ((), (), s32[]{:S(2)}) async-start(), calls=%async_computation.2 | async-start | bytes 1327104 | tf_op jit(solution)/shard_map/all_gather | solution.py:111
  120.2 211.5 %all-reduce.10.cloned.1.call-start = ((), (), s32[]{:S(2)}) async-start(), calls=%async_computation.3 | async-start | bytes 9437184 | tf_op jit(solution)/shard_map/psum | solution.py:147
  213.4 2.1 copy-start
  214.1 2.5 copy-start.28
  237.4 213.0 %all-reduce.12.cloned.1.call-start = ((), (), s32[]{:S(2)}) async-start(), calls=%async_computation.4 | async-start | bytes 9437184 | tf_op jit(solution)/shard_map/psum | solution.py:168
  336.4 1.7 copy-start.3
  340.3 6.5 slice-start
  340.3 6.5 slice-start.2
  340.4 6.5 slice-start.1
  340.4 6.5 slice-start.3
  344.2 2.2 copy-start.2
  344.2 2.7 copy-start.34
  346.9 3.5 copy-start.6
  346.9 4.8 copy-start.33
  350.3 1.4 copy-start.4
  356.0 418.2 %all-reduce.16.cloned.1.call-start = ((), (), s32[]{:S(2)}) async-start(), calls=%async_computation.6 | async-start | bytes 14155776 | tf_op jit(solution)/shard_map/psum | solution.py:215
  356.1 5.3 copy-start.7
  356.1 5.3 copy-start.35
  460.9 2.1 copy-start.1
  538.5 1.4 copy-start.9
  538.5 1.9 copy-start.20
  538.6 331.5 %all-reduce.14.cloned.1.call-start = ((), (), s32[]{:S(2)}) async-start(), calls=%async_computation.5 | async-start | bytes 9437184 | tf_op jit(solution)/shard_map/psum | solution.py:204
  545.0 1.0 copy-start.10
  545.0 1.1 copy-start.15
  545.0 1.3 copy-start.16
  783.6 138.2 %copy-start.14 = (f32[192,96]{1,0:T(8,128)S(1)}, f32[192,96]{1,0:T(8,128)}, u32[]{:S(2)}) copy-start(f32[192,96]{1,0:T(8,128)} %param.34) | copy-start | bytes 221188
  876.6 47.1 %copy-start.11 = (f32[96,768]{1,0:T(8,128)S(1)}, f32[96,768]{1,0:T(8,128)}, u32[]{:S(2)}) copy-start(f32[96,768]{1,0:T(8,128)} %param.35) | copy-start | bytes 884740
  876.6 47.1 %copy-start.17 = (f32[96,768]{1,0:T(8,128)S(1)}, f32[96,768]{1,0:T(8,128)}, u32[]{:S(2)}) copy-start(f32[96,768]{1,0:T(8,128)} %param.39) | copy-start | bytes 884740
  876.6 47.1 %copy-start.18 = (f32[96,768]{1,0:T(8,128)S(1)}, f32[96,768]{1,0:T(8,128)}, u32[]{:S(2)}) copy-start(f32[96,768]{1,0:T(8,128)} %param.43) | copy-start | bytes 884740
  876.6 49.2 %copy-start.12 = (f32[768,96]{0,1:T(8,128)S(1)}, f32[768,96]{0,1:T(8,128)}, u32[]{:S(2)}) copy-start(f32[768,96]{0,1:T(8,128)} %param.36) | copy-start | bytes 884740
  876.6 49.2 %copy-start.19 = (f32[768,96]{0,1:T(8,128)S(1)}, f32[768,96]{0,1:T(8,128)}, u32[]{:S(2)}) copy-start(f32[768,96]{0,1:T(8,128)} %param.40) | copy-start | bytes 884740
  916.9 11.1 %copy-start.27 = (f32[2,192]{1,0:T(2,128)S(1)}, f32[2,192]{1,0:T(2,128)}, u32[]{:S(2)}) copy-start(f32[2,192]{1,0:T(2,128)} %param.45) | copy-start | bytes 4612
  916.9 12.3 %copy-start.23 = (f32[6,768]{1,0:T(8,128)S(1)}, f32[6,768]{1,0:T(8,128)}, u32[]{:S(2)}) copy-start(f32[6,768]{1,0:T(8,128)} %param.47) | copy-start | bytes 55300
  918.3 9.6 %copy-start.31 = (f32[2,192]{1,0:T(2,128)S(1)}, f32[2,192]{1,0:T(2,128)}, u32[]{:S(2)}) copy-start(f32[2,192]{1,0:T(2,128)} %param.48) | copy-start | bytes 4612
  918.3 9.6 %copy-start.32 = (f32[2,192]{1,0:T(2,128)S(1)}, f32[2,192]{1,0:T(2,128)}, u32[]{:S(2)}) copy-start(f32[2,192]{1,0:T(2,128)} %param.51) | copy-start | bytes 4612
  918.3 10.2 %copy-start.29 = (f32[768]{0:T(1024)S(1)}, f32[768]{0:T(1024)}, u32[]{:S(2)}) copy-start(f32[768]{0:T(1024)} %param.49) | copy-start | bytes 9220
  918.3 10.2 %copy-start.30 = (f32[768]{0:T(1024)S(1)}, f32[768]{0:T(1024)}, u32[]{:S(2)}) copy-start(f32[768]{0:T(1024)} %param.52) | copy-start | bytes 9220
  918.3 10.8 %copy-start.24 = (f32[6,768]{1,0:T(8,128)S(1)}, f32[6,768]{1,0:T(8,128)}, u32[]{:S(2)}) copy-start(f32[6,768]{1,0:T(8,128)} %param.50) | copy-start | bytes 55300
  918.3 10.8 %copy-start.25 = (f32[6,768]{1,0:T(8,128)S(1)}, f32[6,768]{1,0:T(8,128)}, u32[]{:S(2)}) copy-start(f32[6,768]{1,0:T(8,128)} %param.53) | copy-start | bytes 55300
Sparse Core Ops, SparseCore 0:
  116.9 93.4 all-reduce.7
  237.5 94.1 all-reduce.9
  356.1 94.1 all-reduce.11
Sparse Core Ops, SparseCore 1:
  120.0 40.8 all-gather.2
  163.5 39.9 all-gather.4
  538.6 235.5 all-reduce.15
  777.3 92.7 all-reduce.13
where the time goes:
time: 947 us; the launch traced here: 938 us
  waiting for transfers between devices  539 us (57%)
  blocking collectives  148 us (16%)
  matrix products  102 us (11%)
  other arithmetic  69.2 us (7%)
  local copies, waits for them, and re-layouts  56 us (6%)
  between operations  22.9 us (2%)
    psum x1, waiting for transfers between devices, on_device(): lax.psum((grad_attn_in, grad_attn_out, grad_ffn_in, grad_ffn_out, grad_qv...  183 us
    psum x1, waiting for transfers between devices, on_device(): ffn_output = lax.psum(ffn_partial, 'tensor') + row_params[4]  94 us
    psum x1, waiting for transfers between devices, on_device(): attended = lax.psum(attn_partial, 'tensor') + row_params[2]  89.9 us
    psum x1, waiting for transfers between devices, on_device(): tokens_grad = grad_res_one + lax.psum(input_part, 'tensor')  86.5 us
    psum x1, waiting for transfers between devices, on_device(): grad_normed = grad_res_two + lax.psum(hidden_part, 'tensor')  85.4 us
    psum x1, blocking collectives, on_device(): total_squares = lax.psum(local_squares, ('dp', 'tensor'))  39.5 us
    psum x1, blocking collectives, on_device(): lax.psum((grad_attn_in, grad_attn_out, grad_ffn_in, grad_ffn_out, grad_qv...  39.3 us
    all_gather x1, blocking collectives, on_device(): lax.all_gather(attn_in_master.astype(jnp.bfloat16), 'dp', axis=1, tiled=T...  38.6 us
  transfers between devices with their start and end apart: 7, of which 5 were waited for; matrix products, arithmetic and copies ran while one was open for 5% of the time, Pallas kernels for 0%

commit v1 on v0

--- a/solution.py
+++ b/solution.py
@@ -248,7 +248,7 @@
     local_squares = local_squares + jnp.sum(small_sums[2] * small_sums[2]) / (
         dp_count * tensor_count
     )
-    total_squares = lax.psum(local_squares, ("dp", "tensor"))
+    total_squares = lax.psum(lax.psum(local_squares, "tensor"), "dp")
     grad_norm = jnp.sqrt(total_squares)
     factor = 1.0 / jnp.maximum(grad_norm, 1.0)
     olds = (

time: 947 us -> 930 us (0.982)
  blocking collectives: 148 us -> 138 us
    psum x1 -> x2, blocking collectives: 39.5 us -> 29.4 us  [on_device(): total_squares = lax.psum(lax.psum(local_squares, 'tensor'), 'dp')]
where the time goes in v1:
time: 930 us; the launch traced here: 921 us
  waiting for transfers between devices  532 us (57%)
  blocking collectives  138 us (15%)
  matrix products  102 us (11%)
  other arithmetic  69.2 us (7%)
  local copies, waits for them, and re-layouts  56 us (6%)
  between operations  22.8 us (2%)
    psum x1, waiting for transfers between devices, on_device(): lax.psum((grad_attn_in, grad_attn_out, grad_ffn_in, grad_ffn_out, grad_qv...  183 us
    psum x1, waiting for transfers between devices, on_device(): ffn_output = lax.psum(ffn_partial, 'tensor') + row_params[4]  94 us
    psum x1, waiting for transfers between devices, on_device(): attended = lax.psum(attn_partial, 'tensor') + row_params[2]  89.9 us
    psum x1, waiting for transfers between devices, on_device(): grad_normed = grad_res_two + lax.psum(hidden_part, 'tensor')  85.4 us
    psum x1, waiting for transfers between devices, on_device(): tokens_grad = grad_res_one + lax.psum(input_part, 'tensor')  79 us
    psum x1, blocking collectives, on_device(): lax.psum((grad_attn_in, grad_attn_out, grad_ffn_in, grad_ffn_out, grad_qv...  39.3 us
    all_gather x1, blocking collectives, on_device(): lax.all_gather(attn_in_master.astype(jnp.bfloat16), 'dp', axis=1, tiled=T...  38.6 us
    all_gather x1, blocking collectives, on_device(): lax.all_gather(attn_out_master.astype(jnp.bfloat16), 'dp', axis=1, tiled=...  31 us
  transfers between devices with their start and end apart: 7, of which 5 were waited for; matrix products, arithmetic and copies ran while one was open for 5% of the time, Pallas kernels for 0%

profile of v1, /device:TPU:0, one launch (start us, length us, event | category | flops | bytes accessed | tf_op | source)
XLA Modules:
  0.0 921.2 jit_solution(10861711040664629021)
XLA Ops:
  9.2 38.6 %all_gather.12 = bf16[3,768,192]{2,0,1:T(4,128)(2,1)S(1)} all-gather(bf16[3,96,192]{2,0,1:T(4,128)(2,1)S(1)} %copy.141), channel_id=1, replica_groups=mesh['dp'=8,'tensor'=4] {'dp'}, dimensions={1}, use_global_device_ids=true | all-gather | bytes 995328 | tf_op jit(solution)/shard_map/all_gather | solution.py:108
  47.8 4.4 convolution_bitcast_fusion.1
  53.4 1.9 squeeze.37
  60.5 6.6 copy.146
  67.2 14.8 %while.28 = (s32[]{:T(128)}, bf16[3,512,3,64]{1,3,2,0:T(8,128)(2,1)S(1)}, f32[3,3,512,1]{2,1,3,0:T(4,128)S(1)}, bf16[3,512,3,64]{1,3,2,0:T(8,128)(2,1)}, s32[3,5...) while((s32[]{:T(128)}, ...), condition=%wide.region_3.4_spmd, body=%wide.region_0.3_spmd.sunk | while | flops 209549824 | bytes 12388973 | solution.py:131
  67.4 2.6 fusion.143
  72.4 2.6 fusion.143
  77.3 2.6 fusion.143
  82.7 31.0 %all_gather.13 = bf16[192,768]{0,1:T(8,128)(2,1)S(1)} all-gather(bf16[192,96]{0,1:T(8,128)(2,1)S(1)} %copy.148), channel_id=1, replica_groups=mesh['dp'=8,'tensor'=4] {'dp'}, dimensions={1}, use_global_device_ids=true | all-gather | bytes 331776 | tf_op jit(solution)/shard_map/all_gather | solution.py:109
  113.7 3.0 fusion.98
  116.8 1.6 convert_element_type.135
  118.5 1.6 convert_element_type.137
  120.5 89.9 %all-reduce.8.cloned.1.call-done = f32[1536,768]{1,0:T(8,128)} async-done(((f32[1536,768]{1,0:T(8,128)}), f32[1536,768]{1,0:T(8,128)}) %all-reduce.8.cloned.1.call-update) | async-done | bytes 4718608 | tf_op jit(solution)/shard_map/psum | solution.py:138
  210.4 3.0 fusion.95
  216.7 14.5 %multiply_convert_fusion.2 = (bf16[1536,768]{1,0:T(8,128)(2,1)}, f32[1536,768]{1,0:T(8,128)}, f32[1536,768]{1,0:T(8,128)}) fusion(f32[768]{0:T(1024)S(1)} %copy-done.28, bf16[1536,768]{1,0:T(8,128)(2,1)S(1)} %fusion.62, bf16[768,768]{1,0:T(8,128)(2,1)} %all-gather.3.cloned.1.call-done), kind=kOutput, calls=%fused_computation.82 | convolution fusion | flops 1889796096 | bytes 15338496 | tf_op jit(solution)/shard_map/dot_general | solution.py:143
  231.2 6.2 fusion.99
  237.7 94.0 %all-reduce.10.cloned.1.call-done = f32[1536,768]{1,0:T(8,128)} async-done(((f32[1536,768]{1,0:T(8,128)}), f32[1536,768]{1,0:T(8,128)}) %all-reduce.10.cloned.1.call-update) | async-done | bytes 4718608 | tf_op jit(solution)/shard_map/psum | solution.py:147
  331.7 4.7 fusion.93
  338.1 2.2 multiply_reduce_fusion.1
  340.4 3.8 fusion.92
  344.2 2.2 copy-done.2
  347.0 3.4 convert_reduce_fusion.2
  351.8 4.2 fusion.100
  356.1 5.3 fusion.102
  361.4 3.6 fusion.103
  365.0 85.4 %all-reduce.12.cloned.1.call-done = f32[1536,768]{1,0:T(8,128)} async-done(((f32[1536,768]{1,0:T(8,128)}), f32[1536,768]{1,0:T(8,128)}) %all-reduce.12.cloned.1.call-update) | async-done | bytes 4718608 | tf_op jit(solution)/shard_map/psum | solution.py:168
  450.3 6.7 multiply_reduce_fusion.2
  457.1 3.8 fusion.91
  468.6 55.0 %while.29 = (s32[]{:T(128)}, bf16[3,512,3,64]{1,3,2,0:T(8,128)(2,1)}, bf16[3,512,3,64]{1,3,2,0:T(8,128)(2,1)}, bf16[3,512,3,64]{1,3,2,0:T(8,128)(2,1)}, f32[3,3,...) while((s32[]{:T(128)}, ...), condition=%wide.region_17.18_spmd, body=%wide.region_15.17_spmd.sunk | while | flops 513505792 | bytes 43427472 | solution.py:176
  470.5 3.0 multiply_reduce_fusion.15
  473.5 2.6 bitcast_convert_fusion.2
  476.1 2.0 fusion.155
  478.1 2.2 fusion.156
  480.3 2.2 fusion.157
  482.5 2.4 copy.203
  484.9 2.0 constant_dynamic-update-slice_fusion.5
  488.8 3.0 multiply_reduce_fusion.15
  491.8 2.6 bitcast_convert_fusion.2
  494.5 2.0 fusion.155
  496.5 2.2 fusion.156
  498.7 2.2 fusion.157
  500.9 2.4 copy.203
  503.3 2.0 constant_dynamic-update-slice_fusion.5
  507.1 3.0 multiply_reduce_fusion.15
  510.2 2.6 bitcast_convert_fusion.2
  512.8 2.0 fusion.155
  514.8 2.2 fusion.156
  517.0 2.2 fusion.157
  519.2 2.4 copy.203
  521.6 2.0 constant_dynamic-update-slice_fusion.5
  533.6 4.9 fusion.66
  540.5 4.5 convolution_bitcast_fusion
  548.0 39.3 %all-reduce = (f32[2,192]{1,0:T(2,128)S(1)}, f32[768]{0:T(1024)S(1)}, f32[6,768]{1,0:T(8,128)S(1)}) all-reduce(f32[2,192]{1,0:T(2,128)S(1)} %pad_maximum_fusion, f32[768]{0:T(1024)S(1)} %get-tuple-element.431, f32[6,768]{1,0:T(8,128)S(1)} %stack.31), channel_id=1, replica_groups=mesh['dp'=8,'tensor'=4] {'dp'}, use_global_device_ids=true, to_apply=%region_29.30 | all-reduce | flops 5760 | bytes 46080 | tf_op jit(solution)/shard_map/psum | solution.py:215
  591.1 183.2 %all-reduce.16.cloned.1.call-done = (f32[3,768,192]{1,2,0:T(8,128)}, f32[192,768]{1,0:T(8,128)}, f32[768,768]{1,0:T(8,128)}, f32[768,768]{0,1:T(8,128)}) async-done(((f32[3,768,192]{1,2,0:T(8,128)}, f32[192,768]{1,0:T(8,128)}, f32[768,768]{1,0:T(8,128)}, f32[768,768]{0,1:T(8,128)}), (f32[3,768,192]{1,2,0:T(8,128)}, f32[192,768]{1,0:T(8,128)}, f32[768,768]{1,0:T(8,128)}, ...) | async-done | bytes 7077904 | tf_op jit(solution)/shard_map/psum | solution.py:215
  775.9 1.8 multiply_reduce_fusion.9
  779.0 1.6 multiply_reduce_fusion.8
  781.3 1.7 multiply_reduce_fusion.7
  783.8 7.4 psum.102
  791.3 79.0 %all-reduce.14.cloned.1.call-done = f32[1536,768]{1,0:T(8,128)} async-done(((f32[1536,768]{1,0:T(8,128)}), f32[1536,768]{1,0:T(8,128)}) %all-reduce.14.cloned.1.call-update) | async-done | bytes 4718608 | tf_op jit(solution)/shard_map/psum | solution.py:204
  870.3 6.5 add_add_fusion.4
  876.8 22.0 %psum.103 = f32[]{:T(128)} all-reduce(f32[]{:T(128)} %psum.102), channel_id=1, replica_groups=mesh['dp'=8,'tensor'=4] {'dp'}, use_global_device_ids=true, to_apply=%region_43.44 | all-reduce | flops 1 | bytes 8 | tf_op jit(solution)/shard_map/psum | solution.py:251
  904.5 1.9 fusion.87
  906.4 2.1 fusion.85
  908.4 2.2 fusion.83
  (202 shorter events, 61.0 us)
Async XLA Ops:
  8.0 202.4 %all-reduce.8.cloned.1.call-start = ((), (), s32[]{:S(2)}) async-start(), calls=%async_computation | async-start | bytes 9437184 | tf_op jit(solution)/shard_map/psum | solution.py:138
  47.8 4.4 copy-start.8
  52.2 3.2 copy-start.26
  60.5 6.7 copy-start.21
  67.2 15.5 %copy-start.13 = (f32[192,96]{1,0:T(8,128)S(1)}, f32[192,96]{1,0:T(8,128)}, u32[]{:S(2)}) copy-start(f32[192,96]{1,0:T(8,128)} %param.34) | copy-start | bytes 221188
  113.7 6.7 copy-start.22
  113.7 96.7 %copy-start.5 = (bf16[1536,768]{1,0:T(8,128)(2,1)S(1)}, bf16[1536,768]{1,0:T(8,128)(2,1)}, u32[]{:S(2)}) copy-start(bf16[1536,768]{1,0:T(8,128)(2,1)} %param.29) | copy-start | bytes 7077892
  116.8 99.9 %all-gather.3.cloned.1.call-start = ((), (), s32[]{:S(2)}) async-start(), calls=%async_computation.1 | async-start | bytes 1327104 | tf_op jit(solution)/shard_map/all_gather | solution.py:110
  118.5 112.7 %all-gather.5.cloned.1.call-start = ((), (), s32[]{:S(2)}) async-start(), calls=%async_computation.2 | async-start | bytes 1327104 | tf_op jit(solution)/shard_map/all_gather | solution.py:111
  120.2 211.5 %all-reduce.10.cloned.1.call-start = ((), (), s32[]{:S(2)}) async-start(), calls=%async_computation.3 | async-start | bytes 9437184 | tf_op jit(solution)/shard_map/psum | solution.py:147
  213.4 2.1 copy-start
  214.1 2.5 copy-start.28
  237.4 213.0 %all-reduce.12.cloned.1.call-start = ((), (), s32[]{:S(2)}) async-start(), calls=%async_computation.4 | async-start | bytes 9437184 | tf_op jit(solution)/shard_map/psum | solution.py:168
  336.4 1.7 copy-start.3
  340.3 6.5 slice-start
  340.3 6.5 slice-start.2
  340.4 6.5 slice-start.1
  340.4 6.5 slice-start.3
  344.2 2.2 copy-start.2
  344.2 2.7 copy-start.34
  346.9 3.5 copy-start.6
  346.9 4.8 copy-start.33
  350.3 1.4 copy-start.4
  356.0 418.3 %all-reduce.16.cloned.1.call-start = ((), (), s32[]{:S(2)}) async-start(), calls=%async_computation.6 | async-start | bytes 14155776 | tf_op jit(solution)/shard_map/psum | solution.py:215
  356.1 5.3 copy-start.7
  356.1 5.3 copy-start.35
  460.9 2.1 copy-start.1
  538.5 1.4 copy-start.9
  538.5 1.9 copy-start.20
  538.6 331.7 %all-reduce.14.cloned.1.call-start = ((), (), s32[]{:S(2)}) async-start(), calls=%async_computation.5 | async-start | bytes 9437184 | tf_op jit(solution)/shard_map/psum | solution.py:204
  545.0 1.0 copy-start.10
  545.0 1.1 copy-start.15
  545.0 238.7 %copy-start.16 = (f32[3,96,192]{2,1,0:T(8,128)S(1)}, f32[3,96,192]{2,1,0:T(8,128)}, u32[]{:S(2)}) copy-start(f32[3,96,192]{2,1,0:T(8,128)} %param.41) | copy-start | bytes 663556
  791.3 113.2 %copy-start.14 = (f32[192,96]{1,0:T(8,128)S(1)}, f32[192,96]{1,0:T(8,128)}, u32[]{:S(2)}) copy-start(f32[192,96]{1,0:T(8,128)} %param.34) | copy-start | bytes 221188
  876.8 29.6 %copy-start.11 = (f32[96,768]{1,0:T(8,128)S(1)}, f32[96,768]{1,0:T(8,128)}, u32[]{:S(2)}) copy-start(f32[96,768]{1,0:T(8,128)} %param.35) | copy-start | bytes 884740
  876.8 29.6 %copy-start.17 = (f32[96,768]{1,0:T(8,128)S(1)}, f32[96,768]{1,0:T(8,128)}, u32[]{:S(2)}) copy-start(f32[96,768]{1,0:T(8,128)} %param.39) | copy-start | bytes 884740
  876.8 29.6 %copy-start.18 = (f32[96,768]{1,0:T(8,128)S(1)}, f32[96,768]{1,0:T(8,128)}, u32[]{:S(2)}) copy-start(f32[96,768]{1,0:T(8,128)} %param.43) | copy-start | bytes 884740
  876.8 31.6 %copy-start.12 = (f32[768,96]{0,1:T(8,128)S(1)}, f32[768,96]{0,1:T(8,128)}, u32[]{:S(2)}) copy-start(f32[768,96]{0,1:T(8,128)} %param.36) | copy-start | bytes 884740
  876.8 31.6 %copy-start.19 = (f32[768,96]{0,1:T(8,128)S(1)}, f32[768,96]{0,1:T(8,128)}, u32[]{:S(2)}) copy-start(f32[768,96]{0,1:T(8,128)} %param.40) | copy-start | bytes 884740
  899.5 11.1 %copy-start.27 = (f32[2,192]{1,0:T(2,128)S(1)}, f32[2,192]{1,0:T(2,128)}, u32[]{:S(2)}) copy-start(f32[2,192]{1,0:T(2,128)} %param.45) | copy-start | bytes 4612
  899.6 12.3 %copy-start.23 = (f32[6,768]{1,0:T(8,128)S(1)}, f32[6,768]{1,0:T(8,128)}, u32[]{:S(2)}) copy-start(f32[6,768]{1,0:T(8,128)} %param.47) | copy-start | bytes 55300
  901.0 9.6 %copy-start.31 = (f32[2,192]{1,0:T(2,128)S(1)}, f32[2,192]{1,0:T(2,128)}, u32[]{:S(2)}) copy-start(f32[2,192]{1,0:T(2,128)} %param.48) | copy-start | bytes 4612
  901.0 9.6 %copy-start.32 = (f32[2,192]{1,0:T(2,128)S(1)}, f32[2,192]{1,0:T(2,128)}, u32[]{:S(2)}) copy-start(f32[2,192]{1,0:T(2,128)} %param.51) | copy-start | bytes 4612
  901.0 10.2 %copy-start.29 = (f32[768]{0:T(1024)S(1)}, f32[768]{0:T(1024)}, u32[]{:S(2)}) copy-start(f32[768]{0:T(1024)} %param.49) | copy-start | bytes 9220
  901.0 10.2 %copy-start.30 = (f32[768]{0:T(1024)S(1)}, f32[768]{0:T(1024)}, u32[]{:S(2)}) copy-start(f32[768]{0:T(1024)} %param.52) | copy-start | bytes 9220
  901.0 10.8 %copy-start.24 = (f32[6,768]{1,0:T(8,128)S(1)}, f32[6,768]{1,0:T(8,128)}, u32[]{:S(2)}) copy-start(f32[6,768]{1,0:T(8,128)} %param.50) | copy-start | bytes 55300
  901.0 10.8 %copy-start.25 = (f32[6,768]{1,0:T(8,128)S(1)}, f32[6,768]{1,0:T(8,128)}, u32[]{:S(2)}) copy-start(f32[6,768]{1,0:T(8,128)} %param.53) | copy-start | bytes 55300
Sparse Core Ops, SparseCore 0:
  116.9 93.4 all-reduce.7
  237.5 94.1 all-reduce.9
  356.1 94.1 all-reduce.11
Sparse Core Ops, SparseCore 1:
  120.0 40.8 all-gather.2
  163.5 39.9 all-gather.4
  538.6 235.6 all-reduce.15
  777.4 92.9 all-reduce.13
